TPU v7x, 128 devices: a whole 4x4x4 slice. The times are simulated.
128 devices in a mesh: gx: 16 (over y, z), gy: 8 (over x, core).
Axes of the slice: x: 4, y: 4, z: 4, core: 2. Of those that a mesh axis runs over, the one named last changes fastest.
Arguments:
- features: bfloat16 [2048, 512, 128], P('gx', 'gy'), may hold values from -6 to 6
- cotangent: bfloat16 [2048, 512, 128], P('gx', 'gy'), may hold values from -31 to 31
- kernel: float32 [7, 7, 128], replicated, may hold values from -0.875 to 0.875
- kernel_bias: float32 [128], replicated, may hold values from -3 to 3
- norm_gain: float32 [128], replicated, may hold values from 0.1 to 1.9
- norm_shift: float32 [128], replicated, may hold values from -3 to 3
- w_up: bfloat16 [128, 512], replicated, may hold values from -0.5 to 0.5
- b_up: float32 [512], replicated, may hold values from -3 to 3
- w_down: bfloat16 [512, 128], replicated, may hold values from -0.25 to 0.25
- b_down: float32 [128], replicated, may hold values from -3 to 3
- layer_scale: float32 [128], replicated, may hold values from 0.3 to 3
Outputs:
- d_features: bfloat16 [2048, 512, 128], P('gx', 'gy')
- d_kernel: float32 [7, 7, 128], replicated
- d_kernel_bias: float32 [128], replicated
- d_norm_gain: float32 [128], replicated
- d_norm_shift: float32 [128], replicated
- d_w_up: float32 [128, 512], replicated
- d_b_up: float32 [512], replicated
- d_w_down: float32 [512, 128], replicated
- d_b_down: float32 [128], replicated
- d_layer_scale: float32 [128], replicated
All inputs are finite; a program needn't handle non-finite values.
Results may differ from a plain program's by a relative error of at most 0.0072.
Values may be sent and summed in bfloat16 or wider, within the bound.
No kernel may reach another device: no remote copies, remote signals or barrier semaphores. Data moves between devices by JAX's collectives and lax.ppermute only.
A program may use at most 64 MiB of HBM per device.

v0:
```python
import math
import jax
import jax.numpy as jnp
from jax import lax
from jax.sharding import PartitionSpec as P

EPSILON = 1e-06


def extended(cells, sides, width):
    for axis, dim in sides:
        count = lax.axis_size(axis)
        head = lax.slice_in_dim(cells, 0, width, axis=dim)
        tail = lax.slice_in_dim(cells, cells.shape[dim] - width, cells.shape[dim], axis=dim)
        cells = jnp.concatenate(
            [
                lax.ppermute(tail, axis, [(i, (i + 1) % count) for i in range(count)]),
                cells,
                lax.ppermute(head, axis, [((i + 1) % count, i) for i in range(count)]),
            ],
            axis=dim,
        )
    return cells


def gelu_pair(hidden):
    erf_part = jax.scipy.special.erf(hidden * 0.7071067811865476)
    value = 0.5 * hidden * (1.0 + erf_part)
    slope_value = (
        0.5 * (1.0 + erf_part) + hidden * jnp.exp(-0.5 * hidden * hidden) * 0.3989422804014327
    )
    return (value, slope_value)


def product(spec, left, right):
    return jnp.einsum(spec, left, right, preferred_element_type=jnp.float32)


def depthwise(padded, kernel, row_count, col_count):
    tap_count = kernel.shape[0]
    accum = jnp.zeros((row_count, col_count, kernel.shape[2]), jnp.float32)
    for row_tap in range(tap_count):
        for col_tap in range(tap_count):
            window = padded[row_tap : row_tap + row_count, col_tap : col_tap + col_count]
            accum = accum + window.astype(jnp.float32) * kernel[row_tap, col_tap]
    return accum


def spread_back(padded, kernel, row_count, col_count):
    tap_count = kernel.shape[0]
    edge_cells = tap_count - 1
    accum = jnp.zeros((row_count, col_count, kernel.shape[2]), jnp.float32)
    for row_tap in range(tap_count):
        for col_tap in range(tap_count):
            window = padded[
                edge_cells - row_tap : edge_cells - row_tap + row_count,
                edge_cells - col_tap : edge_cells - col_tap + col_count,
            ]
            accum = accum + window * kernel[row_tap, col_tap]
    return accum


def kernel_grad(slopes_in, padded, tap_count):
    row_count, col_count = (slopes_in.shape[0], slopes_in.shape[1])
    rows_out = []
    for row_tap in range(tap_count):
        line = []
        for col_tap in range(tap_count):
            window = padded[row_tap : row_tap + row_count, col_tap : col_tap + col_count].astype(
                jnp.float32
            )
            line.append(jnp.sum(slopes_in * window, axis=(0, 1)))
        rows_out.append(jnp.stack(line, 0))
    return jnp.stack(rows_out, 0)


def mask_edges(padded, width):
    col_total = padded.shape[1]
    inner_cols = col_total - 2 * width
    grid_cols = inner_cols * lax.axis_size("gy")
    col_place = lax.axis_index("gy") * inner_cols + lax.iota(jnp.int32, col_total) - width
    keep_mask = (col_place >= 0) & (col_place < grid_cols)
    return jnp.where(keep_mask[None, :, None], padded, jnp.zeros((), padded.dtype))


def layer_back(conv_out, cotan, norm_gain, norm_shift, w_up, b_up, w_down, b_down, layer_scale):
    chan_mean = jnp.mean(conv_out, axis=-1, keepdims=True)
    centred = conv_out - chan_mean
    inv_std = lax.rsqrt(jnp.mean(centred * centred, axis=-1, keepdims=True) + EPSILON)
    normed = centred * inv_std
    normal_out = (normed * norm_gain + norm_shift).astype(jnp.bfloat16)
    hidden = product("rwc,ce->rwe", normal_out, w_up) + b_up
    active, gelu_slope = gelu_pair(hidden)
    active = active.astype(jnp.bfloat16)
    output = product("rwe,ec->rwc", active, w_down) + b_down
    cot_float = cotan.astype(jnp.float32)
    d_output = (cot_float * layer_scale).astype(jnp.bfloat16)
    d_active = product("rwc,ec->rwe", d_output, w_down)
    d_hidden = (d_active * gelu_slope).astype(jnp.bfloat16)
    d_normal = product("rwe,ce->rwc", d_hidden, w_up)
    d_normed = d_normal * norm_gain
    first_mean = jnp.mean(d_normed, axis=-1, keepdims=True)
    second_mean = jnp.mean(d_normed * normed, axis=-1, keepdims=True)
    d_conv = inv_std * (d_normed - first_mean - normed * second_mean)
    d_gain = jnp.sum(d_normal * normed, axis=(0, 1))
    d_shift = jnp.sum(d_normal, axis=(0, 1))
    d_wup = product("rwc,rwe->ce", normal_out, d_hidden)
    d_bup = jnp.sum(d_hidden.astype(jnp.float32), axis=(0, 1))
    d_wdown = product("rwe,rwc->ec", active, d_output)
    d_bdown = jnp.sum(d_output.astype(jnp.float32), axis=(0, 1))
    d_lscale = jnp.sum(cot_float * output, axis=(0, 1))
    return (d_conv, (d_gain, d_shift, d_wup, d_bup, d_wdown, d_bdown, d_lscale))


def local(
    features,
    cotangent,
    kernel,
    kernel_bias,
    norm_gain,
    norm_shift,
    w_up,
    b_up,
    w_down,
    b_down,
    layer_scale,
):
    tap_count = kernel.shape[0]
    reach_cells = tap_count // 2
    row_count, col_count = (features.shape[0], features.shape[1])
    padded_x = mask_edges(extended(features, (("gx", 0), ("gy", 1)), reach_cells), reach_cells)
    conv_out = depthwise(padded_x, kernel, row_count, col_count) + kernel_bias
    d_conv, layer_grads = layer_back(
        conv_out, cotangent, norm_gain, norm_shift, w_up, b_up, w_down, b_down, layer_scale
    )
    d_kern = kernel_grad(d_conv, padded_x, tap_count)
    d_kbias = jnp.sum(d_conv, axis=(0, 1))
    padded_slope = mask_edges(extended(d_conv, (("gx", 0), ("gy", 1)), reach_cells), reach_cells)
    spread = spread_back(padded_slope, kernel, row_count, col_count)
    d_features = (cotangent.astype(jnp.float32) + spread).astype(jnp.bfloat16)
    d_gain, d_shift, d_wup, d_bup, d_wdown, d_bdown, d_lscale = layer_grads
    summed = lax.psum(
        (d_kern, d_kbias, d_gain, d_shift, d_wup, d_bup, d_wdown, d_bdown, d_lscale), ("gx", "gy")
    )
    factor = 1.0 / math.sqrt(row_count * col_count * lax.axis_size("gx") * lax.axis_size("gy"))
    return (d_features,) + tuple((entry * factor for entry in summed))


def solution(mesh):
    placed = (P("gx", "gy", None), P("gx", "gy", None), P(), P(), P(), P(), P(), P(), P(), P(), P())
    return jax.shard_map(
        local,
        mesh=mesh,
        in_specs=placed,
        out_specs=(P("gx", "gy", None), P(), P(), P(), P(), P(), P(), P(), P(), P()),
        check_vma=False,
    )
```

profile of v0, /device:TPU:1, one launch (start us, length us, event | category | flops | bytes accessed | tf_op | source)
XLA Modules:
  0.0 487.0 jit_solution(8291468814353680774)
XLA Ops:
  7.3 3.1 copy.22
  10.4 2.5 collective-permute-start
  13.0 4.9 %collective-permute-start.1 = (bf16[3,64,128]{2,0,1:T(4,128)(2,1)S(1)}, bf16[3,64,128]{2,0,1:T(4,128)(2,1)S(1)}, u32[]{:S(2)}, u32[]{:S(2)}) collective-permute-start(bf16[3,64,128]{2,0,1:T(4,128)(2,1)S(1)} %get-tuple-element.93), channel_id=1, source_target_pairs={{8,0},{16,8},{24,16},{32,24},{40,32},{48,40},{56,48},{64,56},{72,6... | collective-permute-start | bytes 147464 | tf_op jit(solution)/shard_map/ppermute | solution.py:19
  18.0 1.1 convert_reduce_fusion.1
  19.3 2.6 collective-permute-start.2
  21.9 1.7 collective-permute-done.2
  23.6 2.4 collective-permute-done.3
  26.0 2.9 maximum_select_fusion.1
  29.0 33.0 %fusion.163 = (f32[128,64]{0,1:T(8,128)S(1)}, f32[128,64,128]{2,0,1:T(8,128)S(1)}) fusion(f32[128]{0:T(128)S(1)} %copy-done.11, f32[128]{0:T(128)S(1)} %get-tuple-element.141, bf16[134,70,128]{2,0,1:T(8,128)(2,1)S(1)} %maximum_select_fusion.1, f32[128]{0:T(128)S(1)} %get-tuple-element.142, f32[128]{0:T(128)S(1)} %get-tuple-element.95, ...), kind=kLoop, calls=%fused_computation.403 | loop fusion | flops 155181056 | bytes 107013120 | tf_op jit(solution)/shard_map/reduce_sum | solution.py:87
  62.0 2.7 multiply_reduce_fusion.2
  64.8 8.6 %multiply_convert_fusion = (bf16[128,64,512]{2,0,1:T(8,128)(2,1)}, f32[128,64,512]{2,0,1:T(8,128)S(1)}) fusion(f32[512]{0:T(512)S(1)} %copy-done.9, bf16[128,512]{1,0:T(8,128)(2,1)S(1)} %copy-done, f32[128,64,128]{2,0,1:T(8,128)S(1)} %get-tuple-element.85, f32[128]{0:T(128)S(1)} %copy-done.8, f32[128]{0:T(128)S(1)} %copy-done.7, ...), kind=kOutput, calls=%fused_computation.7 | convolution fusion | flops 1104150528 | bytes 29559808 | tf_op jit(solution)/shard_map/rwc,ce->rwe/dot_general | solution.py:36
  73.5 10.9 %convert_reduce_fusion = (f32[512]{0:T(512)S(1)}, bf16[128,64,512]{2,0,1:T(8,128)(2,1)S(1)}) fusion(f32[128,64,512]{2,0,1:T(8,128)S(1)} %get-tuple-element.147, f32[512]{0:T(512)S(1)} %copy-done.9, bf16[512,128]{1,0:T(8,128)(2,1)S(1)} %copy-done.12, f32[128]{0:T(128)S(1)} %copy-done.10, bf16[128,64,128]{2,1,0:T(8,128)(2,1)S(1)} %copy-done.4), kind=kOutput, calls=%fused_computation.8 | convolution fusion | flops 1131412992 | bytes 27398656 | tf_op jit(solution)/shard_map/rwc,ec->rwe/dot_general | solution.py:36
  84.4 4.2 convolution_bitcast_fusion.1
  88.6 4.8 multiply_reduce_fusion
  93.3 13.4 %fusion.102 = (f32[128]{0:T(128)S(1)}, f32[128]{0:T(128)S(1)}, f32[128]{0:T(128)S(1)}, f32[128]{0:T(128)S(1)}, f32[128]{0:T(128)S(1)}, /*index=5*/f32[128]{0:T(1...) fusion(bf16[134,70,128]{2,0,1:T(8,128)(2,1)S(1)} %maximum_selec, ...), kind=kLoop, calls=%fused_computation.208 | loop fusion | flops 63960832 | bytes 50472448 | tf_op jit(solution)/shard_map/reduce_sum | solution.py:72
  106.8 11.0 %fusion.84 = (f32[128]{0:T(128)S(1)}, f32[128]{0:T(128)S(1)}, f32[128]{0:T(128)S(1)}, f32[128]{0:T(128)S(1)}, f32[128]{0:T(128)S(1)}, /*index=5*/f32[128]{0:T(12...) fusion(f32[128,64,128]{2,0,1:T(8,128)S(1)} %get-tuple-element.8, ...), kind=kLoop, calls=%fused_computation.190 | loop fusion | flops 56620800 | bytes 41952256 | tf_op jit(solution)/shard_map/reduce_sum | solution.py:72
  117.8 8.2 %fusion.43 = (f32[128]{0:T(128)S(1)}, f32[128]{0:T(128)S(1)}, f32[128]{0:T(128)S(1)}, f32[128]{0:T(128)S(1)}, f32[128]{0:T(128)S(1)}, /*index=5*/f32[128]{0:T(12...) fusion(f32[128,64,128]{2,0,1:T(8,128)S(1)} %get-tuple-element.8, ...), kind=kLoop, calls=%fused_computation.149 | loop fusion | flops 41941248 | bytes 31464448 | tf_op jit(solution)/shard_map/reduce_sum | solution.py:72
  126.2 4.3 convolution_bitcast_fusion
  130.5 6.2 %fusion.105 = f32[128]{0:T(128)S(1)} fusion(bf16[128,64,512]{2,0,1:T(8,128)(2,1)} %get-tuple-element.146, f32[128]{0:T(128)S(1)} %copy-done.13, bf16[128,64,128]{2,1,0:T(8,128)(2,1)S(1)} %copy-done.5, bf16[512,128]{1,0:T(8,128)(2,1)S(1)} %copy-done.12), kind=kOutput, calls=%fused_computation.211 | convolution fusion | flops 1077936000 | bytes 10617856 | tf_op jit(solution)/shard_map/rwe,ec->rwc/dot_general | solution.py:36
  137.0 67.9 %all-reduce = (f32[7,7,128]{2,1,0:T(8,128)S(1)}, f32[128]{0:T(128)S(1)}, f32[128]{0:T(128)S(1)}, f32[128]{0:T(128)S(1)}, f32[512]{0:T(512)S(1)}, /*index=5*/f32[128]{0:T(128)S(1)}, f32[128]{0:T(128)S(1)}) all-reduce(f32[7,7,128]{2,1,0:T(8,128)S(1)} %constant_dynamic-update-slice_fusion, ...), channel_id=1, replica_groups=mesh['gx'=16,'gy'=8] {'gx','gy'}, use_global_device_ids=true, to_apply=%region_53.54 | all-reduce | flops 7424 | bytes 59392 | tf_op jit(solution)/shard_map/psum | solution.py:142
  204.9 0.6 broadcast_multiply_fusion.5
  208.2 4.8 collective-permute-start.5
  213.5 1.8 collective-permute-done.4
  215.3 1.1 pad_maximum_fusion.2
  216.4 1.5 collective-permute-start.6
  217.9 0.8 collective-permute-start.7
  218.8 136.7 %all-reduce.4.cloned.1.call-done = (f32[128,512]{1,0:T(8,128)}, f32[512,128]{1,0:T(8,128)}) async-done(((f32[128,512]{1,0:T(8,128)}, f32[512,128]{1,0:T(8,128)}), (f32[128,512]{1,0:T(8,128)}, f32[512,128]{1,0:T(8,128)})) %all-reduce.4.cloned.1.call-update) | async-done | bytes 524304 | tf_op jit(solution)/shard_map/psum | solution.py:142
  355.4 1.7 broadcast_multiply_fusion
  357.1 1.7 broadcast_multiply_fusion.1
  358.8 5.5 %maximum_select_fusion = f32[134,70,128]{2,0,1:T(8,128)} fusion(f32[134,3,128]{2,0,1:T(8,128)S(1)} %collective-permute-done.7, f32[3,64,128]{2,0,1:T(4,128)S(1)} %collective-permute-done.5, f32[128,64,128]{2,0,1:T(8,128)} %copy-done.2, f32[3,64,128]{2,0,1:T(4,128)S(1)} %collective-permute-done.4, f32[134,3,128]{2,0,1:T(8,128)S(1)} %collective-permute-done.6, ...), kind=kLoop, calls=%fused_computation.111 | loop fusion | flops 6003200 | bytes 9605190 | tf_op jit(solution)/shard_map/jit(_where)/select_n | solution.py:83
  364.3 111.4 %fusion.104 = bf16[128,64,128]{2,0,1:T(8,128)(2,1)} fusion(f32[134,70,128]{2,0,1:T(8,128)} %maximum_select_fusion, f32[128]{0:T(128)S(1)} %get-tuple-element.141, f32[128]{0:T(128)S(1)} %get-tuple-element.142, f32[128]{0:T(128)S(1)} %get-tuple-element.95, f32[128]{0:T(128)S(1)} %get-tuple-element.96, f32[128]{0:T(128)S(1)} %get-tuple-element.97, ...), kind=kLoop, calls=%fused_computation.210 | loop fusion | flops 104857600 | bytes 209740288 | tf_op jit(solution)/shard_map/convert_element_type | solution.py:140
  475.7 4.3 copy.27
  (72 shorter events, 3.9 us)
Async XLA Ops:
  7.2 57.6 %copy-start = (bf16[128,512]{1,0:T(8,128)(2,1)S(1)}, bf16[128,512]{1,0:T(8,128)(2,1)}, u32[]{:S(2)}) copy-start(bf16[128,512]{1,0:T(8,128)(2,1)} %param.17) | copy-start | bytes 393220
  7.2 10.7 %copy-start.6 = (f32[7,7,128]{2,1,0:T(8,128)S(1)}, f32[7,7,128]{2,1,0:T(8,128)}, u32[]{:S(2)}) copy-start(f32[7,7,128]{2,1,0:T(8,128)} %param.13) | copy-start | bytes 75268
  7.2 10.7 %copy-start.10 = (f32[128]{0:T(128)S(1)}, f32[128]{0:T(128)}, u32[]{:S(2)}) copy-start(f32[128]{0:T(128)} %param.21) | copy-start | bytes 1540
  7.2 348.2 %all-reduce.4.cloned.1.call-start = ((), (), s32[]{:S(2)}) async-start(), calls=%async_computation | async-start | bytes 1048576 | tf_op jit(solution)/shard_map/psum | solution.py:142
  7.3 10.7 %copy-start.3 = (bf16[128,64,128]{2,1,0:T(8,128)(2,1)S(1)}, bf16[128,64,128]{2,1,0:T(8,128)(2,1)}, u32[]{:S(2)}) copy-start(bf16[128,64,128]{2,1,0:T(8,128)(2,1)} %param.12) | copy-start | bytes 6291460
  10.4 8.8 %collective-permute-start = (bf16[3,64,128]{2,0,1:T(4,128)(2,1)S(1)}, bf16[3,64,128]{2,0,1:T(4,128)(2,1)S(1)}, u32[]{:S(2)}, u32[]{:S(2)}) collective-permute-start(bf16[3,64,128]{2,0,1:T(4,128)(2,1)S(1)} %get-tuple-element.92), channel_id=1, source_target_pairs={{0,8},{8,16},{16,24},{24,32},{32,40},{40,48},{48,56},{56,64},{64,7... | collective-permute-start | bytes 147464 | tf_op jit(solution)/shard_map/ppermute | solution.py:17
  13.0 6.3 %collective-permute-start.1 = (bf16[3,64,128]{2,0,1:T(4,128)(2,1)S(1)}, bf16[3,64,128]{2,0,1:T(4,128)(2,1)S(1)}, u32[]{:S(2)}, u32[]{:S(2)}) collective-permute-start(bf16[3,64,128]{2,0,1:T(4,128)(2,1)S(1)} %get-tuple-element.93), channel_id=1, source_target_pairs={{8,0},{16,8},{24,16},{32,24},{40,32},{48,40},{56,48},{64,56},{72,6... | collective-permute-start | bytes 147464 | tf_op jit(solution)/shard_map/ppermute | solution.py:19
  19.1 9.9 %copy-start.11 = (f32[128]{0:T(128)S(1)}, f32[128]{0:T(128)}, u32[]{:S(2)}) copy-start(f32[128]{0:T(128)} %param.14) | copy-start | bytes 1540
  19.3 4.3 collective-permute-start.2
  21.9 4.1 collective-permute-start.3
  62.0 2.8 copy-start.7
  62.0 2.8 copy-start.8
  62.0 2.8 copy-start.9
  64.8 8.7 %copy-start.4 = (bf16[128,64,128]{2,1,0:T(8,128)(2,1)S(1)}, bf16[128,64,128]{2,1,0:T(8,128)(2,1)}, u32[]{:S(2)}) copy-start(bf16[128,64,128]{2,1,0:T(8,128)(2,1)} %param.12) | copy-start | bytes 6291460
  64.8 8.6 %copy-start.12 = (bf16[512,128]{1,0:T(8,128)(2,1)S(1)}, bf16[512,128]{1,0:T(8,128)(2,1)}, u32[]{:S(2)}) copy-start(bf16[512,128]{1,0:T(8,128)(2,1)} %param.19) | copy-start | bytes 393220
  93.3 32.8 %slice-start = ((s8[8388608]{0:T(1024)(128)(4,1)}), s8[4194304]{0:T(1024)(128)(4,1)S(1)}, s32[]{:S(2)}) async-start(s8[8388608]{0:T(1024)(128)(4,1)} %bitcast.185), calls=%async_computation.1 | async-start | bytes 8388608
  106.7 19.3 %copy-start.2 = (f32[128,64,128]{2,0,1:T(8,128)}, f32[128,64,128]{2,0,1:T(8,128)S(1)}, u32[]{:S(2)}) copy-start(f32[128,64,128]{2,0,1:T(8,128)S(1)} %get-tuple-element.83) | copy-start | bytes 12582916
  106.8 19.4 %slice-start.1 = ((s8[8388608]{0:T(1024)(128)(4,1)}), s8[4194304]{0:T(1024)(128)(4,1)S(1)}, s32[]{:S(2)}) async-start(s8[8388608]{0:T(1024)(128)(4,1)} %bitcast.185), calls=%async_computation.2 | async-start | bytes 8388608
  117.8 8.3 %copy-start.5 = (bf16[128,64,128]{2,1,0:T(8,128)(2,1)S(1)}, bf16[128,64,128]{2,1,0:T(8,128)(2,1)}, u32[]{:S(2)}) copy-start(bf16[128,64,128]{2,1,0:T(8,128)(2,1)} %param.12) | copy-start | bytes 6291460
  126.2 4.4 copy-start.13
  208.2 7.1 %collective-permute-start.4 = (f32[3,64,128]{2,0,1:T(4,128)S(1)}, f32[3,64,128]{2,0,1:T(4,128)S(1)}, u32[]{:S(2)}, u32[]{:S(2)}) collective-permute-start(f32[3,64,128]{2,0,1:T(4,128)S(1)} %get-tuple-element.88), channel_id=1, source_target_pairs={{0,8},{8,16},{16,24},{24,32},{32,40},{40,48},{48,56},{56,64},{64,7... | collective-permute-start | bytes 294920 | tf_op jit(solution)/shard_map/ppermute | solution.py:17
  208.2 7.1 %collective-permute-start.5 = (f32[3,64,128]{2,0,1:T(4,128)S(1)}, f32[3,64,128]{2,0,1:T(4,128)S(1)}, u32[]{:S(2)}, u32[]{:S(2)}) collective-permute-start(f32[3,64,128]{2,0,1:T(4,128)S(1)} %get-tuple-element.89), channel_id=1, source_target_pairs={{8,0},{16,8},{24,16},{32,24},{40,32},{48,40},{56,48},{64,56},{72,6... | collective-permute-start | bytes 294920 | tf_op jit(solution)/shard_map/ppermute | solution.py:19
  216.4 142.4 %collective-permute-start.6 = (f32[134,3,128]{2,0,1:T(8,128)S(1)}, f32[134,3,128]{2,0,1:T(8,128)S(1)}, u32[]{:S(2)}, u32[]{:S(2)}) collective-permute-start(f32[134,3,128]{2,0,1:T(8,128)S(1)} %get-tuple-element.86), channel_id=1, source_target_pairs={{0,1},{1,2},{2,3},{3,4},{4,5},{5,6},{6,7},{7,0},{8,9},{9,10},{10,1... | collective-permute-start | bytes 617480 | tf_op jit(solution)/shard_map/ppermute | solution.py:17
  217.9 140.9 %collective-permute-start.7 = (f32[134,3,128]{2,0,1:T(8,128)S(1)}, f32[134,3,128]{2,0,1:T(8,128)S(1)}, u32[]{:S(2)}, u32[]{:S(2)}) collective-permute-start(f32[134,3,128]{2,0,1:T(8,128)S(1)} %get-tuple-element.87), channel_id=1, source_target_pairs={{1,0},{2,1},{3,2},{4,3},{5,4},{6,5},{7,6},{0,7},{9,8},{10,9},{11,1... | collective-permute-start | bytes 617480 | tf_op jit(solution)/shard_map/ppermute | solution.py:19
  364.3 115.7 %copy-start.1 = (bf16[128,512]{1,0:T(8,128)(2,1)S(1)}, bf16[128,512]{1,0:T(8,128)(2,1)}, u32[]{:S(2)}) copy-start(bf16[128,512]{1,0:T(8,128)(2,1)} %param.17) | copy-start | bytes 393220
Sparse Core Ops, SparseCore 0:
  213.1 142.2 all-reduce.3
where the time goes:
time: 490 us; the launch traced here: 487 us
  other arithmetic  198 us (40%)
  waiting for transfers between devices  143 us (29%)
  blocking collectives  67.9 us (14%)
  matrix products  39 us (8%)
  starting transfers between devices  17.3 us (4%)
  between operations  14.7 us (3%)
  local copies, waits for them, and re-layouts  7.79 us (2%)
    psum x1, waiting for transfers between devices, local(): lax.psum((d_kern, d_kbias, d_gain, d_shift, d_wup, d_bup, d_wdown, d_bdow...  137 us
    convert_element_type x1, other arithmetic, local(): d_features = (cotangent.astype(jnp.float32) + spread).astype(jnp.bfloat16)  111 us
    psum x1, blocking collectives, local(): lax.psum((d_kern, d_kbias, d_gain, d_shift, d_wup, d_bup, d_wdown, d_bdow...  67.9 us
    dot_general x6, matrix products, product(): return jnp.einsum(spec, left, right, preferred_element_type=jnp.float32)  39 us
    reduce_sum x1, other arithmetic, layer_back(): chan_mean = jnp.mean(conv_out, axis=-1, keepdims=True)  33 us
    reduce_sum x3, other arithmetic, kernel_grad(): line.append(jnp.sum(slopes_in * window, axis=(0, 1)))  32.6 us
    ppermute x4, starting transfers between devices, extended(): lax.ppermute(head, axis, [((i + 1) % count, i) for i in range(count)])  10.6 us
  transfers between devices with their start and end apart: 9, of which 5 were waited for; matrix products, arithmetic and copies ran while one was open for 1% of the time, Pallas kernels for 0%

commit v1 on v0

--- a/solution.py
+++ b/solution.py
@@ -3,8 +3,15 @@
 import jax.numpy as jnp
 from jax import lax
 from jax.sharding import PartitionSpec as P
+from jax.lax import psum
 
 EPSILON = 1e-06
+
+
+def _drive_quarters(state, mesh_ax, row_axis):
+    for s in (mesh_ax, row_axis):
+        state = psum(state, axis_name=s)
+    return state
 
 
 def extended(cells, sides, width):
@@ -139,8 +146,8 @@
     spread = spread_back(padded_slope, kernel, row_count, col_count)
     d_features = (cotangent.astype(jnp.float32) + spread).astype(jnp.bfloat16)
     d_gain, d_shift, d_wup, d_bup, d_wdown, d_bdown, d_lscale = layer_grads
-    summed = lax.psum(
-        (d_kern, d_kbias, d_gain, d_shift, d_wup, d_bup, d_wdown, d_bdown, d_lscale), ("gx", "gy")
+    summed = _drive_quarters(
+        (d_kern, d_kbias, d_gain, d_shift, d_wup, d_bup, d_wdown, d_bdown, d_lscale), "gx", "gy"
     )
     factor = 1.0 / math.sqrt(row_count * col_count * lax.axis_size("gx") * lax.axis_size("gy"))
     return (d_features,) + tuple((entry * factor for entry in summed))

time: 490 us -> 452 us (0.922)
  waiting for transfers between devices: 143 us -> 75.3 us
  blocking collectives: 67.9 us -> 96.1 us
    psum x1 -> x2, waiting for transfers between devices: 137 us -> 66.7 us  [_drive_quarters(): state = psum(state, axis_name=s)]
    psum x1 -> x2, blocking collectives: 67.9 us -> 96.1 us  [_drive_quarters(): state = psum(state, axis_name=s)]
  transfers between devices with their start and end apart: 9 -> 10, of which waited for: 5 -> 7; matrix products, arithmetic and copies ran while one was open for 1% -> 27% of each run, Pallas kernels for 0% -> 0%
where the time goes in v1:
time: 452 us; the launch traced here: 449 us
  other arithmetic  196 us (43%)
  blocking collectives  96.1 us (21%)
  waiting for transfers between devices  75.3 us (17%)
  matrix products  39 us (9%)
  starting transfers between devices  19.5 us (4%)
  between operations  14.7 us (3%)
  local copies, waits for them, and re-layouts  7.8 us (2%)
    convert_element_type x1, other arithmetic, local(): d_features = (cotangent.astype(jnp.float32) + spread).astype(jnp.bfloat16)  112 us
    psum x2, blocking collectives, _drive_quarters(): state = psum(state, axis_name=s)  96.1 us
    psum x2, waiting for transfers between devices, _drive_quarters(): state = psum(state, axis_name=s)  66.7 us
    dot_general x6, matrix products, product(): return jnp.einsum(spec, left, right, preferred_element_type=jnp.float32)  39 us
    reduce_sum x1, other arithmetic, layer_back(): chan_mean = jnp.mean(conv_out, axis=-1, keepdims=True)  33.1 us
    reduce_sum x3, other arithmetic, kernel_grad(): line.append(jnp.sum(slopes_in * window, axis=(0, 1)))  32.6 us
    ppermute x4, starting transfers between devices, extended(): lax.ppermute(head, axis, [((i + 1) % count, i) for i in range(count)])  11.9 us
  transfers between devices with their start and end apart: 10, of which 7 were waited for; matrix products, arithmetic and copies ran while one was open for 27% of the time, Pallas kernels for 0%

profile of v1, /device:TPU:1, one launch (start us, length us, event | category | flops | bytes accessed | tf_op | source)
XLA Modules:
  0.0 448.6 jit_solution(10525759509758602689)
XLA Ops:
  7.3 3.1 copy.22
  10.4 2.5 collective-permute-start
  13.0 4.9 %collective-permute-start.1 = (bf16[3,64,128]{2,0,1:T(4,128)(2,1)S(1)}, bf16[3,64,128]{2,0,1:T(4,128)(2,1)S(1)}, u32[]{:S(2)}, u32[]{:S(2)}) collective-permute-start(bf16[3,64,128]{2,0,1:T(4,128)(2,1)S(1)} %get-tuple-element.102), channel_id=1, source_target_pairs={{8,0},{16,8},{24,16},{32,24},{40,32},{48,40},{56,48},{64,56},{72,6... | collective-permute-start | bytes 147464 | tf_op jit(solution)/shard_map/ppermute | solution.py:26
  18.0 1.1 convert_reduce_fusion.1
  19.3 2.6 collective-permute-start.2
  21.9 1.7 collective-permute-done.2
  23.6 2.4 collective-permute-done.3
  26.0 2.9 maximum_select_fusion.1
  29.0 33.1 %fusion.163 = (f32[128,64]{0,1:T(8,128)S(1)}, f32[128,64,128]{2,0,1:T(8,128)S(1)}) fusion(f32[128]{0:T(128)S(1)} %copy-done.12, f32[128]{0:T(128)S(1)} %get-tuple-element.150, bf16[134,70,128]{2,0,1:T(8,128)(2,1)S(1)} %maximum_select_fusion.1, f32[128]{0:T(128)S(1)} %get-tuple-element.151, f32[128]{0:T(128)S(1)} %get-tuple-element.104, ...), kind=kLoop, calls=%fused_computation.403 | loop fusion | flops 155181056 | bytes 107013120 | tf_op jit(solution)/shard_map/reduce_sum | solution.py:94
  62.1 2.7 multiply_reduce_fusion.2
  64.9 8.6 %multiply_convert_fusion = (bf16[128,64,512]{2,0,1:T(8,128)(2,1)}, f32[128,64,512]{2,0,1:T(8,128)S(1)}) fusion(f32[512]{0:T(512)S(1)} %copy-done.10, bf16[128,512]{1,0:T(8,128)(2,1)S(1)} %copy-done, f32[128,64,128]{2,0,1:T(8,128)S(1)} %get-tuple-element.94, f32[128]{0:T(128)S(1)} %copy-done.9, f32[128]{0:T(128)S(1)} %copy-done.8, ...), kind=kOutput, calls=%fused_computation.7 | convolution fusion | flops 1104150528 | bytes 29559808 | tf_op jit(solution)/shard_map/rwc,ce->rwe/dot_general | solution.py:43
  73.6 10.9 %convert_reduce_fusion = (f32[512]{0:T(512)S(1)}, bf16[128,64,512]{2,0,1:T(8,128)(2,1)S(1)}) fusion(f32[128,64,512]{2,0,1:T(8,128)S(1)} %get-tuple-element.156, f32[512]{0:T(512)S(1)} %copy-done.10, bf16[512,128]{1,0:T(8,128)(2,1)S(1)} %copy-done.13, f32[128]{0:T(128)S(1)} %copy-done.11, bf16[128,64,128]{2,1,0:T(8,128)(2,1)S(1)} %copy-done.5), kind=kOutput, calls=%fused_computation.8 | convolution fusion | flops 1131412992 | bytes 27398656 | tf_op jit(solution)/shard_map/rwc,ec->rwe/dot_general | solution.py:43
  84.5 4.2 convolution_bitcast_fusion.1
  88.6 4.8 %multiply_reduce_fusion = (f32[128]{0:T(128)S(1)}, f32[128,64]{0,1:T(8,128)S(1)}, f32[128,64]{0,1:T(8,128)S(1)}, f32[128]{0:T(128)S(1)}, f32[128,64,128]{2,0,1:T(8,128)S(1)}) fusion(f32[128,64,128]{2,0,1:T(8,128)S(1)} %get-tuple-element.94, f32[128,64]{0,1:T(8,128)S(1)} %add_rsqrt_fusion, f32[128,64]{0,1:T(8,128)S(1)} %broadcast_multiply_fusion.4, ...), kind=kOutput, calls=%fused_computation.310 | convolution fusion | flops 1083162368 | bytes 17040896 | tf_op jit(solution)/shard_map/rwe,ce->rwc/dot_general | solution.py:43
  93.4 13.4 %fusion.102 = (f32[128]{0:T(128)S(1)}, f32[128]{0:T(128)S(1)}, f32[128]{0:T(128)S(1)}, f32[128]{0:T(128)S(1)}, f32[128]{0:T(128)S(1)}, /*index=5*/f32[128]{0:T(1...) fusion(bf16[134,70,128]{2,0,1:T(8,128)(2,1)S(1)} %maximum_selec, ...), kind=kLoop, calls=%fused_computation.208 | loop fusion | flops 63960832 | bytes 50472448 | tf_op jit(solution)/shard_map/reduce_sum | solution.py:79
  106.8 11.0 %fusion.84 = (f32[128]{0:T(128)S(1)}, f32[128]{0:T(128)S(1)}, f32[128]{0:T(128)S(1)}, f32[128]{0:T(128)S(1)}, f32[128]{0:T(128)S(1)}, /*index=5*/f32[128]{0:T(12...) fusion(f32[128,64,128]{2,0,1:T(8,128)S(1)} %get-tuple-element.9, ...), kind=kLoop, calls=%fused_computation.190 | loop fusion | flops 56620800 | bytes 41952256 | tf_op jit(solution)/shard_map/reduce_sum | solution.py:79
  117.9 8.2 %fusion.43 = (f32[128]{0:T(128)S(1)}, f32[128]{0:T(128)S(1)}, f32[128]{0:T(128)S(1)}, f32[128]{0:T(128)S(1)}, f32[128]{0:T(128)S(1)}, /*index=5*/f32[128]{0:T(12...) fusion(f32[128,64,128]{2,0,1:T(8,128)S(1)} %get-tuple-element.9, ...), kind=kLoop, calls=%fused_computation.149 | loop fusion | flops 41941248 | bytes 31464448 | tf_op jit(solution)/shard_map/reduce_sum | solution.py:79
  126.2 4.3 convolution_bitcast_fusion
  130.6 6.2 %fusion.105 = f32[128]{0:T(128)S(1)} fusion(bf16[128,64,512]{2,0,1:T(8,128)(2,1)} %get-tuple-element.155, f32[128]{0:T(128)S(1)} %copy-done.14, bf16[128,64,128]{2,1,0:T(8,128)(2,1)S(1)} %copy-done.6, bf16[512,128]{1,0:T(8,128)(2,1)S(1)} %copy-done.13), kind=kOutput, calls=%fused_computation.211 | convolution fusion | flops 1077936000 | bytes 10617856 | tf_op jit(solution)/shard_map/rwe,ec->rwc/dot_general | solution.py:43
  137.1 61.2 %all-reduce = (f32[7,7,128]{2,1,0:T(8,128)S(1)}, f32[128]{0:T(128)S(1)}, f32[128]{0:T(128)S(1)}, f32[128]{0:T(128)S(1)}, f32[512]{0:T(512)S(1)}, /*index=5*/f32[128]{0:T(128)S(1)}, f32[128]{0:T(128)S(1)}) all-reduce(f32[7,7,128]{2,1,0:T(8,128)S(1)} %constant_dynamic-update-slice_fusion, ...), channel_id=1, replica_groups=mesh['gx'=16,'gy'=8] {'gx'}, use_global_device_ids=true, to_apply=%region_53.54 | all-reduce | flops 7424 | bytes 59392 | tf_op jit(solution)/shard_map/psum | solution.py:13
  198.2 34.9 %all-reduce.2 = (f32[7,7,128]{2,1,0:T(8,128)S(1)}, f32[128]{0:T(128)S(1)}, f32[128]{0:T(128)S(1)}, f32[128]{0:T(128)S(1)}, f32[512]{0:T(512)S(1)}, /*index=5*/f32[128]{0:T(128)S(1)}, f32[128]{0:T(128)S(1)}) all-reduce(f32[7,7,128]{2,1,0:T(8,128)S(1)} %get-tuple-element.74, ...), channel_id=1, replica_groups=mesh['gx'=16,'gy'=8] {'gy'}, use_global_device_ids=true, to_apply=%region_54.55 | all-reduce | flops 7424 | bytes 59392 | tf_op jit(solution)/shard_map/psum | solution.py:13
  235.9 4.8 %collective-permute-start.5 = (f32[3,64,128]{2,0,1:T(4,128)S(1)}, f32[3,64,128]{2,0,1:T(4,128)S(1)}, u32[]{:S(2)}, u32[]{:S(2)}) collective-permute-start(f32[3,64,128]{2,0,1:T(4,128)S(1)} %get-tuple-element.98), channel_id=1, source_target_pairs={{8,0},{16,8},{24,16},{32,24},{40,32},{48,40},{56,48},{64,56},{72,6... | collective-permute-start | bytes 294920 | tf_op jit(solution)/shard_map/ppermute | solution.py:26
  241.3 1.8 collective-permute-done.4
  244.1 2.4 collective-permute-start.6
  246.5 2.1 collective-permute-start.7
  249.6 2.1 collective-permute-done.7
  251.7 3.8 maximum_select_fusion
  255.6 66.7 %all-reduce.7.cloned.1.call-done = (f32[128,512]{1,0:T(8,128)}, f32[512,128]{1,0:T(8,128)}) async-done(((f32[128,512]{1,0:T(8,128)}, f32[512,128]{1,0:T(8,128)}), (f32[128,512]{1,0:T(8,128)}, f32[512,128]{1,0:T(8,128)})) %all-reduce.7.cloned.1.call-update) | async-done | bytes 524304 | tf_op jit(solution)/shard_map/psum | solution.py:13
  322.3 111.6 %fusion.104 = bf16[128,64,128]{2,0,1:T(8,128)(2,1)} fusion(f32[134,70,128]{2,0,1:T(8,128)} %maximum_select_fusion, f32[128]{0:T(128)S(1)} %get-tuple-element.150, f32[128]{0:T(128)S(1)} %get-tuple-element.151, f32[128]{0:T(128)S(1)} %get-tuple-element.104, f32[128]{0:T(128)S(1)} %get-tuple-element.105, f32[128]{0:T(128)S(1)} %get-tuple-element.106, ...), kind=kLoop, calls=%fused_computation.210 | loop fusion | flops 104857600 | bytes 209740288 | tf_op jit(solution)/shard_map/convert_element_type | solution.py:147
  433.9 4.3 copy.27
  438.2 1.7 broadcast_multiply_fusion
  439.9 1.7 broadcast_multiply_fusion.1
  (78 shorter events, 6.0 us)
Async XLA Ops:
  7.2 57.7 %copy-start = (bf16[128,512]{1,0:T(8,128)(2,1)S(1)}, bf16[128,512]{1,0:T(8,128)(2,1)}, u32[]{:S(2)}) copy-start(bf16[128,512]{1,0:T(8,128)(2,1)} %param.17) | copy-start | bytes 393220
  7.2 10.7 %copy-start.7 = (f32[7,7,128]{2,1,0:T(8,128)S(1)}, f32[7,7,128]{2,1,0:T(8,128)}, u32[]{:S(2)}) copy-start(f32[7,7,128]{2,1,0:T(8,128)} %param.13) | copy-start | bytes 75268
  7.2 10.7 %copy-start.11 = (f32[128]{0:T(128)S(1)}, f32[128]{0:T(128)}, u32[]{:S(2)}) copy-start(f32[128]{0:T(128)} %param.21) | copy-start | bytes 1540
  7.2 315.0 %all-reduce.7.cloned.1.call-start = ((), (), s32[]{:S(2)}) async-start(), calls=%async_computation | async-start | bytes 1048576 | tf_op jit(solution)/shard_map/psum | solution.py:13
  7.3 10.7 %copy-start.4 = (bf16[128,64,128]{2,1,0:T(8,128)(2,1)S(1)}, bf16[128,64,128]{2,1,0:T(8,128)(2,1)}, u32[]{:S(2)}) copy-start(bf16[128,64,128]{2,1,0:T(8,128)(2,1)} %param.12) | copy-start | bytes 6291460
  10.4 8.8 %collective-permute-start = (bf16[3,64,128]{2,0,1:T(4,128)(2,1)S(1)}, bf16[3,64,128]{2,0,1:T(4,128)(2,1)S(1)}, u32[]{:S(2)}, u32[]{:S(2)}) collective-permute-start(bf16[3,64,128]{2,0,1:T(4,128)(2,1)S(1)} %get-tuple-element.101), channel_id=1, source_target_pairs={{0,8},{8,16},{16,24},{24,32},{32,40},{40,48},{48,56},{56,64},{64,7... | collective-permute-start | bytes 147464 | tf_op jit(solution)/shard_map/ppermute | solution.py:24
  13.0 6.3 %collective-permute-start.1 = (bf16[3,64,128]{2,0,1:T(4,128)(2,1)S(1)}, bf16[3,64,128]{2,0,1:T(4,128)(2,1)S(1)}, u32[]{:S(2)}, u32[]{:S(2)}) collective-permute-start(bf16[3,64,128]{2,0,1:T(4,128)(2,1)S(1)} %get-tuple-element.102), channel_id=1, source_target_pairs={{8,0},{16,8},{24,16},{32,24},{40,32},{48,40},{56,48},{64,56},{72,6... | collective-permute-start | bytes 147464 | tf_op jit(solution)/shard_map/ppermute | solution.py:26
  19.1 9.9 %copy-start.12 = (f32[128]{0:T(128)S(1)}, f32[128]{0:T(128)}, u32[]{:S(2)}) copy-start(f32[128]{0:T(128)} %param.14) | copy-start | bytes 1540
  19.3 4.3 collective-permute-start.2
  21.9 4.1 collective-permute-start.3
  62.1 2.8 copy-start.8
  62.1 2.8 copy-start.9
  62.1 2.8 copy-start.10
  64.9 8.7 %copy-start.5 = (bf16[128,64,128]{2,1,0:T(8,128)(2,1)S(1)}, bf16[128,64,128]{2,1,0:T(8,128)(2,1)}, u32[]{:S(2)}) copy-start(bf16[128,64,128]{2,1,0:T(8,128)(2,1)} %param.12) | copy-start | bytes 6291460
  64.9 8.7 %copy-start.13 = (bf16[512,128]{1,0:T(8,128)(2,1)S(1)}, bf16[512,128]{1,0:T(8,128)(2,1)}, u32[]{:S(2)}) copy-start(bf16[512,128]{1,0:T(8,128)(2,1)} %param.19) | copy-start | bytes 393220
  93.4 32.8 %slice-start = ((s8[8388608]{0:T(1024)(128)(4,1)}), s8[4194304]{0:T(1024)(128)(4,1)S(1)}, s32[]{:S(2)}) async-start(s8[8388608]{0:T(1024)(128)(4,1)} %bitcast.185), calls=%async_computation.2 | async-start | bytes 8388608
  106.8 19.3 %copy-start.2 = (f32[128,64,128]{2,0,1:T(8,128)}, f32[128,64,128]{2,0,1:T(8,128)S(1)}, u32[]{:S(2)}) copy-start(f32[128,64,128]{2,0,1:T(8,128)S(1)} %get-tuple-element.92) | copy-start | bytes 12582916
  106.8 19.4 %slice-start.1 = ((s8[8388608]{0:T(1024)(128)(4,1)}), s8[4194304]{0:T(1024)(128)(4,1)S(1)}, s32[]{:S(2)}) async-start(s8[8388608]{0:T(1024)(128)(4,1)} %bitcast.185), calls=%async_computation.3 | async-start | bytes 8388608
  117.9 8.3 %copy-start.6 = (bf16[128,64,128]{2,1,0:T(8,128)(2,1)S(1)}, bf16[128,64,128]{2,1,0:T(8,128)(2,1)}, u32[]{:S(2)}) copy-start(bf16[128,64,128]{2,1,0:T(8,128)(2,1)} %param.12) | copy-start | bytes 6291460
  126.2 4.4 copy-start.14
  235.9 7.1 %collective-permute-start.4 = (f32[3,64,128]{2,0,1:T(4,128)S(1)}, f32[3,64,128]{2,0,1:T(4,128)S(1)}, u32[]{:S(2)}, u32[]{:S(2)}) collective-permute-start(f32[3,64,128]{2,0,1:T(4,128)S(1)} %get-tuple-element.97), channel_id=1, source_target_pairs={{0,8},{8,16},{16,24},{24,32},{32,40},{40,48},{48,56},{56,64},{64,7... | collective-permute-start | bytes 294920 | tf_op jit(solution)/shard_map/ppermute | solution.py:24
  235.9 7.1 %collective-permute-start.5 = (f32[3,64,128]{2,0,1:T(4,128)S(1)}, f32[3,64,128]{2,0,1:T(4,128)S(1)}, u32[]{:S(2)}, u32[]{:S(2)}) collective-permute-start(f32[3,64,128]{2,0,1:T(4,128)S(1)} %get-tuple-element.98), channel_id=1, source_target_pairs={{8,0},{16,8},{24,16},{32,24},{40,32},{48,40},{56,48},{64,56},{72,6... | collective-permute-start | bytes 294920 | tf_op jit(solution)/shard_map/ppermute | solution.py:26
  241.2 197.0 %all-reduce.9.cloned.1.call-start = ((), (), s32[]{:S(2)}) async-start(), calls=%async_computation.1 | async-start | bytes 1048576 | tf_op jit(solution)/shard_map/psum | solution.py:13
  241.3 10.5 %copy-start.3 = (f32[128,64,128]{2,0,1:T(8,128)S(1)}, f32[128,64,128]{2,0,1:T(8,128)}, u32[]{:S(2)}) copy-start(f32[128,64,128]{2,0,1:T(8,128)} %copy-done.2) | copy-start | bytes 12582916
  244.1 5.5 %collective-permute-start.6 = (f32[134,3,128]{2,0,1:T(8,128)S(1)}, f32[134,3,128]{2,0,1:T(8,128)S(1)}, u32[]{:S(2)}, u32[]{:S(2)}) collective-permute-start(f32[134,3,128]{2,0,1:T(8,128)S(1)} %get-tuple-element.95), channel_id=1, source_target_pairs={{0,1},{1,2},{2,3},{3,4},{4,5},{5,6},{6,7},{7,0},{8,9},{9,10},{10,1... | collective-permute-start | bytes 617480 | tf_op jit(solution)/shard_map/ppermute | solution.py:24
  246.5 5.2 %collective-permute-start.7 = (f32[134,3,128]{2,0,1:T(8,128)S(1)}, f32[134,3,128]{2,0,1:T(8,128)S(1)}, u32[]{:S(2)}, u32[]{:S(2)}) collective-permute-start(f32[134,3,128]{2,0,1:T(8,128)S(1)} %get-tuple-element.96), channel_id=1, source_target_pairs={{1,0},{2,1},{3,2},{4,3},{5,4},{6,5},{7,6},{0,7},{9,8},{10,9},{11,1... | collective-permute-start | bytes 617480 | tf_op jit(solution)/shard_map/ppermute | solution.py:26
  322.3 119.3 %copy-start.1 = (bf16[128,512]{1,0:T(8,128)(2,1)S(1)}, bf16[128,512]{1,0:T(8,128)(2,1)}, u32[]{:S(2)}) copy-start(bf16[128,512]{1,0:T(8,128)(2,1)} %param.17) | copy-start | bytes 393220
Sparse Core Ops, SparseCore 0:
  241.3 80.8 all-reduce.6
  324.6 59.6 all-reduce.8
